TPU v7x, 512 devices: a whole 4x8x8 slice. The times are simulated.
512 devices in a mesh: grp: 16 (over y, core), seq: 32 (over z, x).
Axes of the slice: x: 4, y: 8, z: 8, core: 2. Of those that a mesh axis runs over, the one named last changes fastest.
Arguments:
- attention_output: bfloat16 [8192, 8192], P('grp', 'seq'), may hold values from -6 to 6
- output_gradient: bfloat16 [8192, 8192], P('grp', 'seq'), may hold values from -6 to 6
- output_projection_weight: bfloat16 [8192, 8192], P('seq', 'grp'), may hold values from -0.0625 to 0.0625
- tenant_down_factors: bfloat16 [32, 64, 8192], P(None, None, 'seq'), may hold values from -0.0625 to 0.0625
- tenant_up_factors: bfloat16 [32, 64, 8192], P(None, None, 'seq'), may hold values from -0.0625 to 0.0625
- block_tenant_index: int32 [64], replicated, may hold values from 0 to 31, as said below
- block_valid_rows: int32 [64], replicated, may hold values from 16 to 128, as said below
- tenant_output_row: int32 [32], replicated, may hold values from 0 to 31, as said below
Outputs:
- attention_gradient: bfloat16 [8192, 8192], P('grp', 'seq')
- grad_down: float32 [32, 64, 8192], P('grp', None, 'seq')
- grad_up: float32 [32, 64, 8192], P('grp', None, 'seq')
Inputs may be any that keep to these rules, and one draw needn't show every extreme that they name: `block_tenant_index`: the 4 blocks of one group belong to different tenants whose groups tenant_output_row[t] // 2 differ; in every draw one group keeps a tenant of one block of every group. `block_valid_rows`: in every group one block has all 128 rows valid. `tenant_output_row`: A permutation of the tenants.
All inputs are finite; a program needn't handle non-finite values.
Results may differ from a plain program's by a relative error of at most 0.0031.
Values may be sent and summed in bfloat16 or wider, within the bound.
A program may use at most 64 MiB of HBM per device.

v0:
```python
import jax
import jax.numpy as jnp
from jax import lax
from jax.sharding import PartitionSpec as P

BLOCK = 128


adapter_scale = 2.0


def shards(
    attention_output,
    output_gradient,
    output_projection_weight,
    tenant_down_factors,
    tenant_up_factors,
    block_tenant_index,
    block_valid_rows,
    tenant_output_row,
):
    group_index = lax.axis_index("grp")
    rows_group, head_cols = attention_output.shape
    col_width = output_gradient.shape[1]
    blocks = rows_group // BLOCK
    tenants = tenant_output_row.shape[0]
    place_all = jnp.sum(
        jnp.where(
            block_tenant_index[:, None] == jnp.arange(tenants, dtype=jnp.int32)[None, :],
            tenant_output_row[None, :],
            0,
        ),
        axis=1,
    )
    local_tenants = lax.dynamic_slice_in_dim(block_tenant_index, group_index * blocks, blocks)
    my_counts = lax.dynamic_slice_in_dim(block_valid_rows, group_index * blocks, blocks)
    my_places = lax.dynamic_slice_in_dim(place_all, group_index * blocks, blocks)
    positions = jnp.arange(rows_group, dtype=jnp.int32)
    block_of = positions // BLOCK
    limits = jnp.sum(
        jnp.where(
            jnp.arange(blocks, dtype=jnp.int32)[None, :] == block_of[:, None], my_counts[None, :], 0
        ),
        axis=1,
    )
    masked = jnp.where(
        (positions % BLOCK < limits)[:, None], output_gradient, jnp.zeros((), jnp.bfloat16)
    )
    contract_rows = (((1,), (1,)), ((), ()))
    weight_rows = lax.all_gather(output_projection_weight, "grp", axis=1, tiled=True)
    frozen_input_gradient = lax.dot_general(
        lax.all_gather(masked, "seq", axis=1, tiled=True),
        weight_rows,
        contract_rows,
        preferred_element_type=jnp.float32,
    )
    adapter_down_factor = tenant_down_factors[local_tenants]
    adapter_up_factor = tenant_up_factors[local_tenants]
    hidden_row_blocks = attention_output.reshape(blocks, BLOCK, head_cols)
    gradient_row_blocks = masked.reshape(blocks, BLOCK, col_width)
    down_part = jnp.einsum(
        "bkh,brh->bkr", hidden_row_blocks, adapter_down_factor, preferred_element_type=jnp.float32
    )
    grad_part = jnp.einsum(
        "ejz,elz->ejl", gradient_row_blocks, adapter_up_factor, preferred_element_type=jnp.float32
    )
    down_sum, grad_sum = lax.psum((down_part, grad_part), "seq")
    down_rank_product = down_sum.astype(jnp.bfloat16)
    rank_gradient = grad_sum.astype(jnp.bfloat16)
    adapter_branch_term = jnp.einsum(
        "wtf,wfl->wtl", rank_gradient, adapter_down_factor, preferred_element_type=jnp.float32
    ).reshape(rows_group, head_cols)
    attention_gradient = (frozen_input_gradient + adapter_scale * adapter_branch_term).astype(
        jnp.bfloat16
    )
    down_gradient_panel = adapter_scale * jnp.einsum(
        "eit,eiz->etz", rank_gradient, hidden_row_blocks, preferred_element_type=jnp.float32
    )
    up_gradient_panel = adapter_scale * jnp.einsum(
        "jlx,jln->jxn", down_rank_product, gradient_row_blocks, preferred_element_type=jnp.float32
    )
    panels = jnp.concatenate([down_gradient_panel, up_gradient_panel], axis=2)
    select = (jnp.arange(tenants, dtype=jnp.int32)[:, None] == my_places[None, :]).astype(
        jnp.float32
    )
    spread = jnp.einsum(
        "pb,brx->prx",
        select,
        panels,
        precision=lax.Precision.HIGHEST,
        preferred_element_type=jnp.float32,
    )
    summed = lax.psum_scatter(spread, "grp", scatter_dimension=0, tiled=True)
    grad_down = summed[:, :, :head_cols]
    grad_up = summed[:, :, head_cols:]
    return (attention_gradient, grad_down, grad_up)


def solution(mesh):
    placed = (
        P("grp", "seq"),
        P("grp", "seq"),
        P("seq", "grp"),
        P(None, None, "seq"),
        P(None, None, "seq"),
        P(),
        P(),
        P(),
    )
    return jax.shard_map(
        shards,
        mesh=mesh,
        in_specs=placed,
        out_specs=(P("grp", "seq"), P("grp", None, "seq"), P("grp", None, "seq")),
        check_vma=False,
    )
```

profile of v0, /device:TPU:48, one launch (start us, length us, event | category | flops | bytes accessed | tf_op | source)
XLA Modules:
  0.0 402.9 jit_solution(14572246744692483261)
XLA Ops:
  7.2 0.0 copy-start
  7.2 0.0 reduce-scatter.2.cloned.1.call-start
  7.2 0.8 dynamic_slice.9
  8.1 0.1 select_reduce_fusion.1
  8.1 0.7 compare_select_fusion
  8.9 1.1 broadcast_select_fusion
  10.0 0.0 copy-start.1
  10.0 0.0 copy-done
  10.0 0.6 gather_fusion
  10.6 0.2 fusion.16
  10.8 1.8 gather_fusion.1
  12.6 1.1 convolution_bitcast_fusion
  13.7 150.4 %all-reduce.2 = (bf16[4,128,64]{1,2,0:T(8,128)(2,1)S(1)}, bf16[4,128,64]{1,2,0:T(8,128)(2,1)S(1)}) all-reduce(f32[4,128,64]{1,2,0:T(8,128)S(1)} %fusion.16, f32[4,128,64]{1,2,0:T(8,128)S(1)} %convolution_bitcast_fusion), channel_id=1, replica_groups=mesh['grp'=16,'seq'=32] {'seq'}, use_global_device_ids=true, to_apply=%region_1.2 | all-reduce | flops 65536 | bytes 393216 | tf_op jit(solution)/shard_map/psum | solution.py:67
  164.1 0.2 convolution_multiply_fusion.1
  164.3 1.1 convolution_multiply_fusion.2
  165.4 0.8 select_reduce_fusion
  166.2 0.1 dynamic_slice.11
  166.3 0.1 pad_maximum_fusion
  166.3 2.0 fusion.1
  168.3 0.0 copy-done.1
  168.3 4.4 %copy.15 = f32[32,64,512]{2,1,0:T(8,128)} copy(f32[32,64,512]{2,0,1:T(8,128)S(1)} %fusion.1) | data formatting | bytes 8388608 | tf_op jit(solution)/shard_map/pb,brx->prx/dot_general | solution.py:86
  172.7 0.0 reduce-scatter.2.cloned.1.call-update
  172.7 0.0 all-gather.5.cloned.1.call-start
  172.8 0.7 all-gather.5.cloned.1.call-update
  173.5 0.0 all-gather.3.cloned.1.call-start
  173.5 0.7 all-gather.3.cloned.1.call-update
  174.2 0.3 convolution_multiply_fusion
  174.5 51.9 %reduce-scatter.2.cloned.1.call-done = f32[2,64,512]{2,1,0:T(8,128)} async-done(((f32[32,64,512]{2,1,0:T(8,128)}), f32[2,64,512]{2,1,0:T(8,128)}) %reduce-scatter.2.cloned.1.call-update) | async-done | bytes 262160 | tf_op jit(solution)/shard_map/reduce_scatter | solution.py:93
  226.4 1.7 fusion.15
  228.0 48.4 %all-gather.5.cloned.1.call-done = bf16[256,8192]{1,0:T(8,128)(2,1)} async-done(((bf16[256,512]{1,0:T(8,128)(2,1)}), bf16[256,8192]{1,0:T(8,128)(2,1)}) %all-gather.5.cloned.1.call-update) | async-done | bytes 4194320 | tf_op jit(solution)/shard_map/all_gather | solution.py:50
  276.4 112.3 %all-gather.3.cloned.1.call-done = bf16[512,8192]{1,0:T(8,128)(2,1)} async-done(((bf16[512,256]{1,0:T(8,128)(2,1)}), bf16[512,8192]{1,0:T(8,128)(2,1)}) %all-gather.3.cloned.1.call-update) | async-done | bytes 8388624 | tf_op jit(solution)/shard_map/all_gather | solution.py:52
  388.7 7.6 %fusion = bf16[512,256]{1,0:T(8,128)(2,1)} fusion(f32[512,256]{1,0:T(8,128)S(1)} %bitcast.24, bf16[512,8192]{1,0:T(8,128)(2,1)} %all-gather.3.cloned.1.call-done, bf16[256,8192]{1,0:T(8,128)(2,1)} %all-gather.5.cloned.1.call-done), kind=kOutput, calls=%fused_computation.4 | convolution fusion | flops 2147745792 | bytes 13369344 | tf_op jit(solution)/shard_map/dot_general | solution.py:51
  (3 shorter events, 0.0 us)
Async XLA Ops:
  7.2 2.8 copy-start
  7.2 219.2 %reduce-scatter.2.cloned.1.call-start = ((), (), s32[]{:S(2)}) async-start(), calls=%async_computation.3 | async-start | bytes 4456448 | tf_op jit(solution)/shard_map/reduce_scatter | solution.py:93
  10.0 158.3 %copy-start.1 = (bf16[512,256]{1,0:T(8,128)(2,1)}, bf16[512,256]{1,0:T(8,128)(2,1)S(1)}, u32[]{:S(2)}) copy-start(bf16[512,256]{1,0:T(8,128)(2,1)S(1)} %broadcast_select_fusion) | copy-start | bytes 786436
  172.7 103.7 %all-gather.5.cloned.1.call-start = ((), (), s32[]{:S(2)}) async-start(), calls=%async_computation.2 | async-start | bytes 4456448 | tf_op jit(solution)/shard_map/all_gather | solution.py:50
  173.5 215.2 %all-gather.3.cloned.1.call-start = ((), (), s32[]{:S(2)}) async-start(), calls=%async_computation.1 | async-start | bytes 8650752 | tf_op jit(solution)/shard_map/all_gather | solution.py:52
Sparse Core Ops, SparseCore 0:
  172.8 53.4 reduce-scatter.1
  228.5 47.8 all-gather.4
  280.0 108.6 all-gather.2
where the time goes:
time: 404 us; the launch traced here: 403 us
  waiting for transfers between devices  214 us (53%)
  blocking collectives  150 us (37%)
  between operations  13.9 us (3%)
  matrix products  12.5 us (3%)
  local copies, waits for them, and re-layouts  9.3 us (2%)
    psum x1, blocking collectives, shards(): down_sum, grad_sum = lax.psum((down_part, grad_part), 'seq')  150 us
    all_gather x1, waiting for transfers between devices, shards(): lax.all_gather(masked, 'seq', axis=1, tiled=True)  112 us
    reduce_scatter x1, waiting for transfers between devices, shards(): summed = lax.psum_scatter(spread, 'grp', scatter_dimension=0, tiled=True)  51.9 us
    all_gather x1, waiting for transfers between devices, shards(): lax.all_gather(output_projection_weight, 'grp', axis=1, tiled=True)  48.4 us
  transfers between devices with their start and end apart: 3, of which 3 were waited for; matrix products, arithmetic and copies ran while one was open for 0% of the time, Pallas kernels for 0%

commit v1 on v0

v1 whole, which is shorter than its diff:
```python
import jax
import jax.numpy as jnp
from jax import lax
from jax.experimental import pallas as pl
from jax.experimental.pallas import tpu as pltpu
from jax.sharding import PartitionSpec as P

MESH = pl.DeviceIdType.MESH
F32 = jnp.float32
BF16 = jnp.bfloat16
BLOCK = 128
NB = 4
NY, NZ, NX = 8, 8, 4
RANK = 64
SCALE = 2.0
WIDE = 256
HOPS = ((4, 3), (3, 4))


def wrap(value, size):
    return lax.rem(value + 2 * size, size)


def kernel(
    tenant_ref,
    valid_ref,
    place_ref,
    a_ref,
    g_ref,
    w_ref,
    down_ref,
    up_ref,
    out_ref,
    grad_down_ref,
    grad_up_ref,
    masked,
    m_all,
    w_all,
    partial,
    rank_part,
    rank_x,
    rank_mid,
    rank_z,
    rank_all,
    panels,
    y_send,
    y_recv,
    x_relay,
    x_sum,
    x_in,
    adapter,
    pre_s,
    pre_r,
    w_s,
    w_r,
    sib_s,
    sib_r,
    m_s,
    m_r,
    rx_s,
    rx_r,
    rz_s,
    rz_r,
    gz_s,
    gz_r,
    gx_s,
    gx_r,
    pan_s,
    pan_r,
    ys_s,
    ys_r,
    xs_s,
    xs_r,
    loc_s,
):
    grp, seq = lax.axis_index("grp"), lax.axis_index("seq")
    y, c = lax.div(grp, 2), lax.rem(grp, 2)
    z, x = lax.div(seq, NX), lax.rem(seq, NX)
    other = 1 - c
    sib_grp = y * 2 + other

    def at(yy, cc, zz, xx):
        return (yy * 2 + cc, zz * NX + xx)

    sibling = at(y, other, z, x)
    y_next = (at(wrap(y + 1, NY), c, z, x), at(wrap(y - 1, NY), c, z, x))
    z_next = (at(y, c, wrap(z + 1, NZ), x), at(y, c, wrap(z - 1, NZ), x))
    x_peer = [at(y, c, z, wrap(x + k, NX)) for k in range(1, NX)]
    z_peer = [at(y, c, wrap(z + k, NZ), x) for k in range(1, NZ)]

    sends = []

    def send(src, dst, ssem, rsem, device):
        copy = pltpu.make_async_remote_copy(
            src_ref=src,
            dst_ref=dst,
            send_sem=ssem,
            recv_sem=rsem,
            device_id=device,
            device_id_type=MESH,
        )
        copy.start()
        sends.append(copy)
        return copy

    barrier = pltpu.get_barrier_semaphore()
    greeted = list(x_peer) + list(z_peer) + list(y_next) + [sibling]
    greeted += [at(y, other, z, wrap(x + k, NX)) for k in range(1, NX)]
    for device in greeted:
        pl.semaphore_signal(barrier, inc=1, device_id=device, device_id_type=MESH)
    pl.semaphore_wait(barrier, len(greeted))

    to_core = lax.div(x, 2)
    pre = []
    for j in range(2):
        to_x = 2 * c + j
        is_self = jnp.logical_and(to_x == x, to_core == c)
        piece = w_ref.at[:, pl.ds(j * WIDE, WIDE)]
        spot = w_all.at[y, x]
        keep = pltpu.make_async_copy(piece, spot, pre_r.at[lax.rem(x, 2)])
        move = pltpu.make_async_remote_copy(
            src_ref=piece,
            dst_ref=spot,
            send_sem=pre_s.at[j],
            recv_sem=pre_r.at[lax.rem(x, 2)],
            device_id=at(y, to_core, z, to_x),
            device_id_type=MESH,
        )
        pre.append((is_self, move))

        @pl.when(is_self)
        def _(keep=keep):
            keep.start()

        @pl.when(jnp.logical_not(is_self))
        def _(move=move):
            move.start()

    m_copy = {}

    def m_hop(direction, half, hop):
        owner = wrap(z - hop if direction == 0 else z + hop, NZ)
        src = g_ref.at[pl.ds(half * WIDE, WIDE)] if hop == 0 else m_all.at[owner, half]
        m_copy[direction, half, hop] = send(
            src,
            m_all.at[owner, half],
            m_s.at[direction, half, hop],
            m_r.at[direction, half, hop],
            z_next[direction],
        )

    for half in range(2):
        for direction in range(2):
            m_hop(direction, half, 0)
    own = [
        pltpu.make_async_copy(
            g_ref.at[pl.ds(half * WIDE, WIDE)], m_all.at[z, half], loc_s.at[half]
        )
        for half in range(2)
    ]
    for copy in own:
        copy.start()

    tenants = [tenant_ref[grp * NB + b] for b in range(NB)]
    zeros = jnp.zeros((RANK, WIDE), BF16)
    contract_last = (((1,), (1,)), ((), ()))
    contract_first = (((0,), (0,)), ((), ()))
    row = lax.broadcasted_iota(jnp.int32, (BLOCK, WIDE), 0)
    for b in range(NB):
        rows = pl.ds(b * BLOCK, BLOCK)
        kept = jnp.where(
            row < valid_ref[grp * NB + b], g_ref[rows, :].astype(F32), 0.0
        ).astype(BF16)
        masked[rows, :] = kept
        ups = jnp.concatenate([up_ref[tenants[b]], zeros], axis=0)
        downs = jnp.concatenate([zeros, down_ref[tenants[b]]], axis=0)
        rank_part[b] = lax.dot_general(
            kept, ups, contract_last, preferred_element_type=F32
        ) + lax.dot_general(a_ref[rows, :], downs, contract_last, preferred_element_type=F32)
    rx = []
    for k in range(1, NX):
        rx.append(
            send(
                rank_part.at[wrap(x + k, NX)],
                rank_x.at[k - 1],
                rx_s.at[k - 1],
                rx_r.at[k - 1],
                x_peer[k - 1],
            )
        )
    for shard in range(NX):
        partial[shard] = jnp.zeros((2 * WIDE, WIDE), F32)
    panels[8] = jnp.zeros((RANK, 2 * WIDE), F32)

    w_copy, sib_copy = {}, {}

    def w_hop(direction, j, hop):
        owner = wrap(y - hop if direction == 0 else y + hop, NY)
        spot = w_all.at[owner, 2 * c + j]
        w_copy[direction, j, hop] = send(
            spot, spot, w_s.at[direction, j, hop], w_r.at[direction, j, hop], y_next[direction]
        )

    def to_sibling(owner, slot, j):
        spot = w_all.at[owner, 2 * c + j]
        sib_copy[slot, j] = send(spot, spot, sib_s.at[slot, j], sib_r.at[slot, j], sibling)

    for j in range(2):
        pltpu.make_async_copy(
            w_ref.at[:, pl.ds(0, WIDE)], w_all.at[y, 2 * c + j], pre_r.at[j]
        ).wait()
        for direction in range(2):
            w_hop(direction, j, 0)
        to_sibling(y, 0, j)

    def w_step(hop):
        for j in range(2):
            for direction in range(2):
                last = HOPS[j][direction]
                if hop >= last:
                    continue
                w_copy[direction, j, hop].wait_recv()
                if hop + 1 < last:
                    w_hop(direction, j, hop + 1)
                owner = wrap(y - 1 - hop if direction == 0 else y + 1 + hop, NY)
                to_sibling(owner, w_slot(direction, hop), j)

    def w_slot(direction, hop):
        return 7 if hop == 3 else 1 + 2 * hop + direction

    def m_step(hop):
        for half in range(2):
            for direction in range(2):
                last = HOPS[half][direction]
                if hop >= last:
                    continue
                m_copy[direction, half, hop].wait_recv()
                if hop + 1 < last:
                    m_hop(direction, half, hop + 1)

    for copy in rx:
        copy.wait_recv()
    summed = rank_part[x] + rank_x[0] + rank_x[1] + rank_x[2]
    rank_mid[...] = summed.reshape(NZ, BLOCK // NZ, BLOCK)
    rz = []
    for k in range(1, NZ):
        rz.append(
            send(
                rank_mid.at[wrap(z + k, NZ)],
                rank_z.at[k - 1],
                rz_s.at[k - 1],
                rz_r.at[k - 1],
                z_peer[k - 1],
            )
        )
    m_step(0)
    w_step(0)
    for copy in rz:
        copy.wait_recv()
    total = rank_mid[z]
    for k in range(NZ - 1):
        total = total + rank_z[k]
    rank_all[x, z] = total.astype(BF16)
    gz = []
    for k in range(1, NZ):
        gz.append(
            send(
                rank_all.at[x, z],
                rank_all.at[x, z],
                gz_s.at[k - 1],
                gz_r.at[k - 1],
                z_peer[k - 1],
            )
        )
    m_step(1)
    for copy in gz:
        copy.wait_recv()
    gx = []
    for k in range(1, NX):
        gx.append(
            send(
                rank_all.at[x], rank_all.at[x], gx_s.at[k - 1], gx_r.at[k - 1], x_peer[k - 1]
            )
        )
    w_step(1)
    for copy in gx:
        copy.wait_recv()

    for b in range(NB):
        rows = pl.ds(b * BLOCK, BLOCK)
        ranks = rank_all[b].reshape(BLOCK, BLOCK)
        by_a = lax.dot_general(
            ranks, a_ref[rows, :], contract_first, preferred_element_type=F32
        )
        by_g = lax.dot_general(
            ranks, masked[rows, :], contract_first, preferred_element_type=F32
        )
        panels[b, :, pl.ds(0, WIDE)] = SCALE * by_a[:RANK]
        panels[b, :, pl.ds(WIDE, WIDE)] = SCALE * by_g[RANK:]
    swap = send(
        panels.at[pl.ds(0, NB)], panels.at[pl.ds(NB, NB)], pan_s, pan_r, sibling
    )
    for b in range(NB):
        rows = pl.ds(b * BLOCK, BLOCK)
        ranks = rank_all[b].reshape(BLOCK, BLOCK)
        downs = jnp.concatenate([down_ref[tenants[b]], zeros], axis=0)
        adapter[rows, :] = SCALE * jnp.dot(ranks, downs, preferred_element_type=F32)
    m_step(2)

    my_places = [place_ref[tenants[b]] for b in range(NB)]
    sib_places = [place_ref[tenant_ref[sib_grp * NB + b]] for b in range(NB)]

    def contribution(chip, slot):
        place = 2 * (2 * chip + c) + slot
        mine = theirs = 8
        for b in range(NB):
            mine = jnp.where(my_places[b] == place, b, mine)
            theirs = jnp.where(sib_places[b] == place, NB + b, theirs)
        return panels[mine] + panels[theirs]

    y_copy = {}

    def y_hop(direction, slot, hop):
        distance = HOPS[slot][direction] - hop
        chip = wrap(y + distance if direction == 0 else y - distance, NY)
        value = contribution(chip, slot)
        if hop > 0:
            value = value + y_recv[direction, slot, hop - 1]
        y_send[direction, slot, hop] = value
        y_copy[direction, slot, hop] = send(
            y_send.at[direction, slot, hop],
            y_recv.at[direction, slot, hop],
            ys_s.at[direction, slot, hop],
            ys_r.at[direction, slot, hop],
            y_next[direction],
        )

    def y_step(hop):
        for slot in range(2):
            for direction in range(2):
                if hop + 1 < HOPS[slot][direction]:
                    y_copy[direction, slot, hop].wait_recv()
                    y_hop(direction, slot, hop + 1)

    w_step(2)
    swap.wait_recv()
    for slot in range(2):
        for direction in range(2):
            y_hop(direction, slot, 0)
    m_step(3)
    for copy in own:
        copy.wait()
    for slot in range(5):
        for j in range(2):
            sib_copy[slot, j].wait_recv()

    def multiply(chip, shard):
        partial[shard] += lax.dot_general(
            m_all[chip].reshape(2 * WIDE, WIDE),
            w_all[chip, shard],
            contract_last,
            preferred_element_type=F32,
        )

    def near(n, carry):
        multiply(wrap(y + lax.div(n, NX) - 2, NY), lax.rem(n, NX))
        return carry

    lax.fori_loop(0, 5 * NX, near, 0)
    w_step(3)
    for slot in (5, 6):
        for j in range(2):
            sib_copy[slot, j].wait_recv()

    def far(n, carry):
        multiply(wrap(y + 3 + 2 * lax.div(n, NX), NY), lax.rem(n, NX))
        return carry

    lax.fori_loop(0, 2 * NX, far, 0)
    for j in range(2):
        sib_copy[7, j].wait_recv()
    last_chip = wrap(y + 4, NY)

    x_next = (x_peer[0], x_peer[2])
    x_at = (wrap(x + 1, NX), wrap(x - 1, NX))
    opposite = wrap(x + 2, NX)
    x_copy = {}
    multiply(last_chip, opposite)
    for sub in range(2):
        for direction in range(2):
            rows = pl.ds(direction * WIDE + sub * BLOCK, BLOCK)
            x_copy[0, direction, sub] = send(
                partial.at[opposite, rows],
                x_relay.at[direction, sub],
                xs_s.at[0, direction, sub],
                xs_r.at[0, direction, sub],
                x_next[direction],
            )
    for direction in range(2):
        multiply(last_chip, x_at[direction])
        for sub in range(2):
            rows = pl.ds((1 - direction) * WIDE + sub * BLOCK, BLOCK)
            x_copy[1, direction, sub] = send(
                partial.at[x_at[direction], rows],
                x_in.at[0, direction, sub],
                xs_s.at[1, direction, sub],
                xs_r.at[1, direction, sub],
                x_next[direction],
            )
    multiply(last_chip, x)
    y_step(0)
    for sub in range(2):
        for direction in range(2):
            x_copy[0, direction, sub].wait_recv()
            rows = pl.ds(direction * WIDE + sub * BLOCK, BLOCK)
            x_sum[direction, sub] = x_relay[direction, sub] + partial[x_at[direction], rows, :]
            x_copy[2, direction, sub] = send(
                x_sum.at[direction, sub],
                x_in.at[1, direction, sub],
                xs_s.at[2, direction, sub],
                xs_r.at[2, direction, sub],
                x_next[direction],
            )
    y_step(1)
    y_step(2)
    for direction in range(2):
        for sub in range(2):
            x_copy[1, direction, sub].wait_recv()
    for sub in range(2):
        for half in range(2):
            x_copy[2, half, sub].wait_recv()
            b = half * 2 + sub
            rows = pl.ds(b * BLOCK, BLOCK)
            value = partial[x, rows, :] + x_in[1, half, sub] + x_in[0, 1 - half, sub]
            value = jnp.where(row < valid_ref[grp * NB + b], value, 0.0)
            out_ref[rows, :] = (value + adapter[rows, :]).astype(BF16)
    for slot in range(2):
        total = contribution(y, slot)
        for direction in range(2):
            last = HOPS[slot][direction] - 1
            y_copy[direction, slot, last].wait_recv()
            total = total + y_recv[direction, slot, last]
        grad_down_ref[slot] = total[:, :WIDE]
        grad_up_ref[slot] = total[:, WIDE:]
    for copy in sends:
        copy.wait_send()
    for is_self, move in pre:

        @pl.when(jnp.logical_not(is_self))
        def _(move=move):
            move.wait_send()


def solution(mesh):
    placed = (
        P("grp", "seq"),
        P("grp", "seq"),
        P("seq", "grp"),
        P(None, None, "seq"),
        P(None, None, "seq"),
        P(),
        P(),
        P(),
    )

    def step(a, g, w, down, up, tenants, valid, places):
        vmem = pl.BlockSpec(memory_space=pltpu.VMEM)
        smem = pl.BlockSpec(memory_space=pltpu.SMEM)
        dma = pltpu.SemaphoreType.DMA
        return pl.pallas_call(
            kernel,
            out_shape=(
                jax.ShapeDtypeStruct((NB * BLOCK, WIDE), BF16),
                jax.ShapeDtypeStruct((2, RANK, WIDE), F32),
                jax.ShapeDtypeStruct((2, RANK, WIDE), F32),
            ),
            in_specs=[smem] * 3 + [vmem] * 5,
            out_specs=(vmem, vmem, vmem),
            scratch_shapes=[
                pltpu.VMEM((NB * BLOCK, WIDE), BF16),
                pltpu.VMEM((NZ, 2, WIDE, WIDE), BF16),
                pltpu.VMEM((NY, NX, WIDE, WIDE), BF16),
                pltpu.VMEM((NX, NB * BLOCK, WIDE), F32),
                pltpu.VMEM((NB, BLOCK, BLOCK), F32),
                pltpu.VMEM((NX - 1, BLOCK, BLOCK), F32),
                pltpu.VMEM((NZ, BLOCK // NZ, BLOCK), F32),
                pltpu.VMEM((NZ - 1, BLOCK // NZ, BLOCK), F32),
                pltpu.VMEM((NX, NZ, BLOCK // NZ, BLOCK), BF16),
                pltpu.VMEM((9, RANK, 2 * WIDE), F32),
                pltpu.VMEM((2, 2, 4, RANK, 2 * WIDE), F32),
                pltpu.VMEM((2, 2, 4, RANK, 2 * WIDE), F32),
                pltpu.VMEM((2, 2, BLOCK, WIDE), F32),
                pltpu.VMEM((2, 2, BLOCK, WIDE), F32),
                pltpu.VMEM((2, 2, 2, BLOCK, WIDE), F32),
                pltpu.VMEM((NB * BLOCK, WIDE), F32),
                dma((2,)),
                dma((2,)),
                dma((2, 2, 4)),
                dma((2, 2, 4)),
                dma((8, 2)),
                dma((8, 2)),
                dma((2, 2, 4)),
                dma((2, 2, 4)),
                dma((NX - 1,)),
                dma((NX - 1,)),
                dma((NZ - 1,)),
                dma((NZ - 1,)),
                dma((NZ - 1,)),
                dma((NZ - 1,)),
                dma((NX - 1,)),
                dma((NX - 1,)),
                dma,
                dma,
                dma((2, 2, 4)),
                dma((2, 2, 4)),
                dma((3, 2, 2)),
                dma((3, 2, 2)),
                dma((2,)),
            ],
            compiler_params=pltpu.CompilerParams(
                collective_id=0, has_side_effects=True, vmem_limit_bytes=56 << 20
            ),
        )(tenants, valid, places, a, g, w, down, up)

    return jax.shard_map(
        step,
        mesh=mesh,
        in_specs=placed,
        out_specs=(P("grp", "seq"), P("grp", None, "seq"), P("grp", None, "seq")),
        check_vma=False,
    )
```

time: 404 us -> 79.3 us (0.20)
  the two profiles are of different devices: /device:TPU:48 before, /device:TPU:16 now
where the time goes in v1:
time: 79.3 us; the launch traced here: 79.1 us
  Pallas kernels  75.1 us (95%)
  local copies, waits for them, and re-layouts  3.31 us (4%)
    pallas_call x1, Pallas kernels, step(): pl.pallas_call(kernel, out_shape=(jax.ShapeDtypeStruct((NB * BLOCK, WIDE)...  75.1 us
    unnamed x7, local copies, waits for them, and re-layouts  3.31 us

profile of v1, /device:TPU:16, one launch (start us, length us, event | category | flops | bytes accessed | tf_op | source)
XLA Modules:
  0.0 79.1 jit_solution(17307492834621392217)
XLA Ops:
  0.6 75.1 %shard_map.103 = (bf16[512,256]{1,0:T(8,128)(2,1)}, f32[2,64,256]{2,1,0:T(8,128)}, f32[2,64,256]{2,1,0:T(8,128)}) custom-call(s32[64]{0:T(128)} %tenant_ref.1, s32[64]{0:T(128)} %valid_ref.1, s32[32]{0:T(128)} %place_ref.1, bf16[512,256]{1,0:T(8,128)(2,1)} %a_ref.1, bf16[512,256]{1,0:T(8,128)(2,1)} %g_ref.1, bf16[256,512]{1,0:T(8,128)(2,1)} %w_ref.1, ...), custom_call_target="tpu_custom_call" | custom-call | tf_op jit(solution)/shard_map/pallas_call | solution.py:470
  75.8 0.0 copy-start.1
  75.8 1.7 %copy.14 = bf16[512,256]{1,0:T(8,128)(2,1)} copy(bf16[512,256]{1,0:T(8,128)(2,1)} %get-tuple-element.6) | data formatting | bytes 524288
  77.5 0.0 copy-done.1
  77.5 0.0 copy-start
  77.5 0.7 copy.15
  78.1 0.3 copy-done
  78.4 0.7 copy.16
Async XLA Ops:
  75.8 1.7 %copy-start.1 = (f32[2,64,256]{2,1,0:T(8,128)S(1)}, f32[2,64,256]{2,1,0:T(8,128)}, u32[]{:S(2)}) copy-start(f32[2,64,256]{2,1,0:T(8,128)} %get-tuple-element.7) | copy-start | bytes 393220
  77.5 1.0 %copy-start = (f32[2,64,256]{2,1,0:T(8,128)S(1)}, f32[2,64,256]{2,1,0:T(8,128)}, u32[]{:S(2)}) copy-start(f32[2,64,256]{2,1,0:T(8,128)} %get-tuple-element.8) | copy-start | bytes 393220

commit v2 on v1

v2 whole, which is shorter than its diff:
```python
import jax
import jax.numpy as jnp
from jax import lax
from jax.experimental import pallas as pl
from jax.experimental.pallas import tpu as pltpu
from jax.sharding import PartitionSpec as P

MESH = pl.DeviceIdType.MESH
F32 = jnp.float32
BF16 = jnp.bfloat16
BLOCK = 128
NB = 4
NY, NZ, NX = 8, 8, 4
RANK = 64
SCALE = 2.0
WIDE = 256
Y_TYPE = BF16
X_TYPE = BF16
X_SUM = F32
HOPS = ((4, 3), (3, 4))


def wrap(value, size):
    return lax.rem(value + 2 * size, size)


def kernel(
    tenant_ref,
    valid_ref,
    place_ref,
    a_hbm,
    g_hbm,
    w_hbm,
    down_hbm,
    up_hbm,
    out_ref,
    grad_down_ref,
    grad_up_ref,
    a_ref,
    g_ref,
    w_ref,
    down_ref,
    up_ref,
    masked,
    m_all,
    w_all,
    partial,
    rank_part,
    rank_x,
    rank_mid,
    rank_z,
    rank_all,
    panels,
    y_send,
    y_recv,
    x_out,
    x_relay,
    x_sum,
    x_direct,
    x_far,
    adapter,
    pre_s,
    pre_r,
    w_s,
    w_r,
    sib_s,
    sib_r,
    m_s,
    m_r,
    rx_s,
    rx_r,
    rz_s,
    rz_r,
    gz_s,
    gz_r,
    gx_s,
    gx_r,
    pan_s,
    pan_r,
    ys_s,
    ys_r,
    xs_s,
    xs_r,
    loc_s,
    load_s,
):
    grp, seq = lax.axis_index("grp"), lax.axis_index("seq")
    y, c = lax.div(grp, 2), lax.rem(grp, 2)
    z, x = lax.div(seq, NX), lax.rem(seq, NX)
    other = 1 - c
    sib_grp = y * 2 + other

    def at(yy, cc, zz, xx):
        return (yy * 2 + cc, zz * NX + xx)

    sibling = at(y, other, z, x)
    y_next = (at(wrap(y + 1, NY), c, z, x), at(wrap(y - 1, NY), c, z, x))
    z_next = (at(y, c, wrap(z + 1, NZ), x), at(y, c, wrap(z - 1, NZ), x))
    x_peer = [at(y, c, z, wrap(x + k, NX)) for k in range(1, NX)]
    z_peer = [at(y, c, wrap(z + k, NZ), x) for k in range(1, NZ)]

    sends = []

    def send(src, dst, ssem, rsem, device):
        copy = pltpu.make_async_remote_copy(
            src_ref=src,
            dst_ref=dst,
            send_sem=ssem,
            recv_sem=rsem,
            device_id=device,
            device_id_type=MESH,
        )
        copy.start()
        sends.append(copy)
        return copy

    loads = [
        pltpu.make_async_copy(src, dst, load_s.at[n])
        for n, (src, dst) in enumerate(
            (
                (g_hbm, g_ref),
                (up_hbm, up_ref),
                (a_hbm, a_ref),
                (down_hbm, down_ref),
                (w_hbm, w_ref),
            )
        )
    ]
    for copy in loads:
        copy.start()

    barrier = pltpu.get_barrier_semaphore()
    greeted = list(x_peer) + list(z_peer) + list(y_next) + [sibling]
    greeted += [at(y, other, z, wrap(x + k, NX)) for k in range(1, NX)]
    for device in greeted:
        pl.semaphore_signal(barrier, inc=1, device_id=device, device_id_type=MESH)

    tenants = [tenant_ref[grp * NB + b] for b in range(NB)]
    zeros = jnp.zeros((RANK, WIDE), BF16)
    contract_last = (((1,), (1,)), ((), ()))
    contract_first = (((0,), (0,)), ((), ()))
    row = lax.broadcasted_iota(jnp.int32, (BLOCK, WIDE), 0)
    panels[8] = jnp.zeros((RANK, 2 * WIDE), F32)
    for copy in loads:
        copy.wait()
    own = [
        pltpu.make_async_copy(
            g_ref.at[pl.ds(half * WIDE, WIDE)], m_all.at[z, half], loc_s.at[half]
        )
        for half in range(2)
    ]
    for copy in own:
        copy.start()
    for b in range(NB):
        rows = pl.ds(b * BLOCK, BLOCK)
        kept = jnp.where(
            row < valid_ref[grp * NB + b], g_ref[rows, :].astype(F32), 0.0
        ).astype(BF16)
        masked[rows, :] = kept
        ups = jnp.concatenate([up_ref[tenants[b]], zeros], axis=0)
        downs = jnp.concatenate([zeros, down_ref[tenants[b]]], axis=0)
        rank_part[b] = lax.dot_general(
            kept, ups, contract_last, preferred_element_type=F32
        ) + lax.dot_general(a_ref[rows, :], downs, contract_last, preferred_element_type=F32)
    pl.semaphore_wait(barrier, len(greeted))

    def flip_of(xx, cc):
        low = lax.rem(xx, 2)
        return jnp.where(lax.div(xx, 2) == cc, low, 1 - low)

    flip = flip_of(x, c)

    def shard_of(j):
        return 2 * c + lax.rem(j + flip, 2)

    to_core = lax.div(x, 2)
    pre = []
    for j in range(2):
        to_x = 2 * c + j
        is_self = jnp.logical_and(to_x == x, to_core == c)
        piece = w_ref.at[:, pl.ds(j * WIDE, WIDE)]
        spot = w_all.at[y, x]
        chunk = lax.rem(x + flip_of(to_x, to_core), 2)
        keep = pltpu.make_async_copy(piece, spot, pre_r.at[chunk])
        move = pltpu.make_async_remote_copy(
            src_ref=piece,
            dst_ref=spot,
            send_sem=pre_s.at[j],
            recv_sem=pre_r.at[chunk],
            device_id=at(y, to_core, z, to_x),
            device_id_type=MESH,
        )
        pre.append((is_self, move))

        @pl.when(is_self)
        def _(keep=keep):
            keep.start()

        @pl.when(jnp.logical_not(is_self))
        def _(move=move):
            move.start()

    m_copy, w_copy, sib_copy = {}, {}, {}

    def m_hop(direction, half, hop):
        owner = wrap(z - hop if direction == 0 else z + hop, NZ)
        src = g_ref.at[pl.ds(half * WIDE, WIDE)] if hop == 0 else m_all.at[owner, half]
        m_copy[direction, half, hop] = send(
            src,
            m_all.at[owner, half],
            m_s.at[direction, half, hop],
            m_r.at[direction, half, hop],
            z_next[direction],
        )

    def w_hop(direction, j, hop):
        owner = wrap(y - hop if direction == 0 else y + hop, NY)
        spot = w_all.at[owner, shard_of(j)]
        w_copy[direction, j, hop] = send(
            spot, spot, w_s.at[direction, j, hop], w_r.at[direction, j, hop], y_next[direction]
        )

    def to_sibling(owner, slot, j):
        spot = w_all.at[owner, shard_of(j)]
        sib_copy[slot, j] = send(spot, spot, sib_s.at[slot, j], sib_r.at[slot, j], sibling)

    def w_slot(direction, hop):
        return 7 if hop == 3 else 1 + 2 * hop + direction

    def step(hop):
        for j in range(2):
            for direction in range(2):
                last = HOPS[j][direction]
                if hop >= last:
                    continue
                w_copy[direction, j, hop].wait_recv()
                if hop + 1 < last:
                    w_hop(direction, j, hop + 1)
                owner = wrap(y - 1 - hop if direction == 0 else y + 1 + hop, NY)
                to_sibling(owner, w_slot(direction, hop), j)
                m_copy[direction, j, hop].wait_recv()
                if hop + 1 < last:
                    m_hop(direction, j, hop + 1)

    rx = []
    for k in range(1, NX):
        rx.append(
            send(
                rank_part.at[wrap(x + k, NX)],
                rank_x.at[k - 1],
                rx_s.at[k - 1],
                rx_r.at[k - 1],
                x_peer[k - 1],
            )
        )
    for half in range(2):
        for direction in range(2):
            m_hop(direction, half, 0)
    for j in range(2):
        pltpu.make_async_copy(
            w_ref.at[:, pl.ds(0, WIDE)], w_all.at[y, shard_of(j)], pre_r.at[j]
        ).wait()
        for direction in range(2):
            w_hop(direction, j, 0)
        to_sibling(y, 0, j)
    for shard in range(NX):
        partial[shard] = jnp.zeros((2 * WIDE, WIDE), F32)

    def multiply(chip, shard):
        partial[shard] += lax.dot_general(
            m_all[chip].reshape(2 * WIDE, WIDE),
            w_all[chip, shard],
            contract_last,
            preferred_element_type=F32,
        )

    def ring_distance(a, b, size):
        ahead = wrap(a - b, size)
        return jnp.minimum(ahead, size - ahead)

    def arrived(hop):
        if hop < 0:
            slots = (0,)
        elif hop < 3:
            slots = (1 + 2 * hop, 2 + 2 * hop)
        else:
            slots = (7,)
        for slot in slots:
            for j in range(2):
                sib_copy[slot, j].wait_recv()

    def products(farthest):
        def one(chip, carry):
            far = jnp.maximum(ring_distance(chip, y, NY), ring_distance(chip, z, NZ))

            @pl.when(far == farthest)
            def _():
                for shard in range(NX):
                    multiply(chip, shard)

            return carry

        lax.fori_loop(0, NY, one, 0)

    for copy in rx:
        copy.wait_recv()
    summed = rank_part[x] + rank_x[0] + rank_x[1] + rank_x[2]
    rank_mid[...] = summed.reshape(NZ, BLOCK // NZ, BLOCK)
    rz = []
    for k in range(1, NZ):
        rz.append(
            send(
                rank_mid.at[wrap(z + k, NZ)],
                rank_z.at[k - 1],
                rz_s.at[k - 1],
                rz_r.at[k - 1],
                z_peer[k - 1],
            )
        )
    step(0)
    for copy in own:
        copy.wait()
    arrived(-1)
    products(0)
    for copy in rz:
        copy.wait_recv()
    total = rank_mid[z]
    for k in range(NZ - 1):
        total = total + rank_z[k]
    rank_all[x, z] = total.astype(BF16)
    gz = []
    for k in range(1, NZ):
        gz.append(
            send(
                rank_all.at[x, z],
                rank_all.at[x, z],
                gz_s.at[k - 1],
                gz_r.at[k - 1],
                z_peer[k - 1],
            )
        )
    step(1)
    arrived(0)
    products(1)
    for copy in gz:
        copy.wait_recv()
    gx = []
    for k in range(1, NX):
        gx.append(
            send(
                rank_all.at[x], rank_all.at[x], gx_s.at[k - 1], gx_r.at[k - 1], x_peer[k - 1]
            )
        )
    step(2)
    arrived(1)
    products(2)
    for copy in gx:
        copy.wait_recv()

    for b in range(NB):
        rows = pl.ds(b * BLOCK, BLOCK)
        ranks = rank_all[b].reshape(BLOCK, BLOCK)
        by_a = lax.dot_general(
            ranks, a_ref[rows, :], contract_first, preferred_element_type=F32
        )
        by_g = lax.dot_general(
            ranks, masked[rows, :], contract_first, preferred_element_type=F32
        )
        panels[b, :, pl.ds(0, WIDE)] = SCALE * by_a[:RANK]
        panels[b, :, pl.ds(WIDE, WIDE)] = SCALE * by_g[RANK:]
    swap = send(
        panels.at[pl.ds(0, NB)], panels.at[pl.ds(NB, NB)], pan_s, pan_r, sibling
    )
    for b in range(NB):
        rows = pl.ds(b * BLOCK, BLOCK)
        ranks = rank_all[b].reshape(BLOCK, BLOCK)
        downs = jnp.concatenate([down_ref[tenants[b]], zeros], axis=0)
        adapter[rows, :] = SCALE * jnp.dot(ranks, downs, preferred_element_type=F32)

    my_places = [place_ref[tenants[b]] for b in range(NB)]
    sib_places = [place_ref[tenant_ref[sib_grp * NB + b]] for b in range(NB)]

    def contribution(chip, slot):
        place = 2 * (2 * chip + c) + slot
        mine = theirs = 8
        for b in range(NB):
            mine = jnp.where(my_places[b] == place, b, mine)
            theirs = jnp.where(sib_places[b] == place, NB + b, theirs)
        return panels[mine] + panels[theirs]

    y_copy = {}

    def y_hop(direction, slot, hop):
        distance = HOPS[slot][direction] - hop
        chip = wrap(y + distance if direction == 0 else y - distance, NY)
        value = contribution(chip, slot)
        if hop > 0:
            value = value + y_recv[direction, slot, hop - 1].astype(F32)
        y_send[direction, slot, hop] = value.astype(Y_TYPE)
        y_copy[direction, slot, hop] = send(
            y_send.at[direction, slot, hop],
            y_recv.at[direction, slot, hop],
            ys_s.at[direction, slot, hop],
            ys_r.at[direction, slot, hop],
            y_next[direction],
        )

    def y_step(hop):
        for slot in range(2):
            for direction in range(2):
                if hop + 1 < HOPS[slot][direction]:
                    y_copy[direction, slot, hop].wait_recv()
                    y_hop(direction, slot, hop + 1)

    swap.wait_recv()
    for slot in range(2):
        for direction in range(2):
            y_hop(direction, slot, 0)
    step(3)
    arrived(2)
    products(3)
    arrived(3)
    x_next = (x_peer[0], x_peer[2])
    x_at = (wrap(x + 1, NX), wrap(x - 1, NX))
    opposite = wrap(x + 2, NX)
    x_copy = {}

    for shard in range(NX):
        multiply(wrap(y + 4, NY), shard)

    @pl.when(y != z)
    def _():
        for shard in range(NX):
            multiply(wrap(z + 4, NZ), shard)

    def x_send(kind, direction, sub, src, dst):
        x_copy[kind, direction, sub] = send(
            src,
            dst,
            xs_s.at[kind, direction, sub],
            xs_r.at[kind, direction, sub],
            x_next[direction],
        )

    for sub in range(2):
        for direction in range(2):
            rows = pl.ds(direction * WIDE + sub * BLOCK, BLOCK)
            x_out[0, direction, sub] = partial[opposite, rows, :].astype(X_TYPE)
            x_send(0, direction, sub, x_out.at[0, direction, sub], x_relay.at[direction, sub])
    for direction in range(2):
        for sub in range(2):
            rows = pl.ds((1 - direction) * WIDE + sub * BLOCK, BLOCK)
            x_out[1, direction, sub] = partial[x_at[direction], rows, :].astype(X_TYPE)
            x_send(1, direction, sub, x_out.at[1, direction, sub], x_direct.at[direction, sub])
    y_step(0)
    for sub in range(2):
        for direction in range(2):
            x_copy[0, direction, sub].wait_recv()
            rows = pl.ds(direction * WIDE + sub * BLOCK, BLOCK)
            value = x_relay[direction, sub].astype(F32) + partial[x_at[direction], rows, :]
            x_sum[direction, sub] = value.astype(X_SUM)
            x_send(2, direction, sub, x_sum.at[direction, sub], x_far.at[direction, sub])
    y_step(1)
    y_step(2)
    for direction in range(2):
        for sub in range(2):
            x_copy[1, direction, sub].wait_recv()
    for sub in range(2):
        for half in range(2):
            x_copy[2, half, sub].wait_recv()
            b = half * 2 + sub
            rows = pl.ds(b * BLOCK, BLOCK)
            value = (
                partial[x, rows, :]
                + x_far[half, sub].astype(F32)
                + x_direct[1 - half, sub].astype(F32)
            )
            value = jnp.where(row < valid_ref[grp * NB + b], value, 0.0)
            out_ref[rows, :] = (value + adapter[rows, :]).astype(BF16)
    for slot in range(2):
        total = contribution(y, slot)
        for direction in range(2):
            last = HOPS[slot][direction] - 1
            y_copy[direction, slot, last].wait_recv()
            total = total + y_recv[direction, slot, last].astype(F32)
        grad_down_ref[slot] = total[:, :WIDE]
        grad_up_ref[slot] = total[:, WIDE:]
    for copy in sends:
        copy.wait_send()
    for is_self, move in pre:

        @pl.when(jnp.logical_not(is_self))
        def _(move=move):
            move.wait_send()


def solution(mesh):
    placed = (
        P("grp", "seq"),
        P("grp", "seq"),
        P("seq", "grp"),
        P(None, None, "seq"),
        P(None, None, "seq"),
        P(),
        P(),
        P(),
    )

    def whole(a, g, w, down, up, tenants, valid, places):
        vmem = pl.BlockSpec(memory_space=pltpu.VMEM)
        smem = pl.BlockSpec(memory_space=pltpu.SMEM)
        hbm = pl.BlockSpec(memory_space=pltpu.HBM)
        dma = pltpu.SemaphoreType.DMA
        return pl.pallas_call(
            kernel,
            out_shape=(
                pltpu.VMEM((NB * BLOCK, WIDE), BF16),
                pltpu.VMEM((2, RANK, WIDE), F32),
                pltpu.VMEM((2, RANK, WIDE), F32),
            ),
            in_specs=[smem] * 3 + [hbm] * 5,
            out_specs=(vmem, vmem, vmem),
            scratch_shapes=[
                pltpu.VMEM((NB * BLOCK, WIDE), BF16),
                pltpu.VMEM((NB * BLOCK, WIDE), BF16),
                pltpu.VMEM((WIDE, 2 * WIDE), BF16),
                pltpu.VMEM(down.shape, BF16),
                pltpu.VMEM(up.shape, BF16),
                pltpu.VMEM((NB * BLOCK, WIDE), BF16),
                pltpu.VMEM((NZ, 2, WIDE, WIDE), BF16),
                pltpu.VMEM((NY, NX, WIDE, WIDE), BF16),
                pltpu.VMEM((NX, NB * BLOCK, WIDE), F32),
                pltpu.VMEM((NB, BLOCK, BLOCK), F32),
                pltpu.VMEM((NX - 1, BLOCK, BLOCK), F32),
                pltpu.VMEM((NZ, BLOCK // NZ, BLOCK), F32),
                pltpu.VMEM((NZ - 1, BLOCK // NZ, BLOCK), F32),
                pltpu.VMEM((NX, NZ, BLOCK // NZ, BLOCK), BF16),
                pltpu.VMEM((9, RANK, 2 * WIDE), F32),
                pltpu.VMEM((2, 2, 4, RANK, 2 * WIDE), Y_TYPE),
                pltpu.VMEM((2, 2, 4, RANK, 2 * WIDE), Y_TYPE),
                pltpu.VMEM((2, 2, 2, BLOCK, WIDE), X_TYPE),
                pltpu.VMEM((2, 2, BLOCK, WIDE), X_TYPE),
                pltpu.VMEM((2, 2, BLOCK, WIDE), X_SUM),
                pltpu.VMEM((2, 2, BLOCK, WIDE), X_TYPE),
                pltpu.VMEM((2, 2, BLOCK, WIDE), X_SUM),
                pltpu.VMEM((NB * BLOCK, WIDE), F32),
                dma((2,)),
                dma((2,)),
                dma((2, 2, 4)),
                dma((2, 2, 4)),
                dma((8, 2)),
                dma((8, 2)),
                dma((2, 2, 4)),
                dma((2, 2, 4)),
                dma((NX - 1,)),
                dma((NX - 1,)),
                dma((NZ - 1,)),
                dma((NZ - 1,)),
                dma((NZ - 1,)),
                dma((NZ - 1,)),
                dma((NX - 1,)),
                dma((NX - 1,)),
                dma,
                dma,
                dma((2, 2, 4)),
                dma((2, 2, 4)),
                dma((3, 2, 2)),
                dma((3, 2, 2)),
                dma((2,)),
                dma((5,)),
            ],
            compiler_params=pltpu.CompilerParams(
                collective_id=0, has_side_effects=True, vmem_limit_bytes=56 << 20
            ),
        )(tenants, valid, places, a, g, w, down, up)

    return jax.shard_map(
        whole,
        mesh=mesh,
        in_specs=placed,
        out_specs=(P("grp", "seq"), P("grp", None, "seq"), P("grp", None, "seq")),
        check_vma=False,
    )
```

time: 79.3 us -> 65.8 us (0.83)
  Pallas kernels: 75.1 us -> 63 us
  local copies, waits for them, and re-layouts: 3.31 us -> 2.01 us
    pallas_call x1, Pallas kernels: 75.1 us -> 63 us  [whole(): pl.pallas_call(kernel, out_shape=(pltpu.VMEM((NB * BLOCK, WIDE), BF16), p...]
    unnamed x7 -> x3, local copies, waits for them, and re-layouts: 3.31 us -> 2.01 us
where the time goes in v2:
time: 65.8 us; the launch traced here: 65.7 us
  Pallas kernels  63 us (96%)
  local copies, waits for them, and re-layouts  2.01 us (3%)
    pallas_call x1, Pallas kernels, whole(): pl.pallas_call(kernel, out_shape=(pltpu.VMEM((NB * BLOCK, WIDE), BF16), p...  63 us
    unnamed x3, local copies, waits for them, and re-layouts  2.01 us

profile of v2, /device:TPU:16, one launch (start us, length us, event | category | flops | bytes accessed | tf_op | source)
XLA Modules:
  0.0 65.7 jit_solution(4797923197261485298)
XLA Ops:
  0.6 63.0 %shard_map.103 = (bf16[512,256]{1,0:T(8,128)(2,1)S(1)}, f32[2,64,256]{2,1,0:T(8,128)S(1)}, f32[2,64,256]{2,1,0:T(8,128)S(1)}) custom-call(s32[64]{0:T(128)} %tenant_ref.1, s32[64]{0:T(128)} %valid_ref.1, s32[32]{0:T(128)} %place_ref.1, bf16[512,256]{1,0:T(8,128)(2,1)} %a_hbm.1, bf16[512,256]{1,0:T(8,128)(2,1)} %g_hbm.1, bf16[256,512]{1,0:T(8,128)(2,1)} %w_hbm.1, ...), custom_call_target="tpu_custom_call" | custom-call | tf_op jit(solution)/shard_map/pallas_call | solution.py:514
  63.6 0.7 %copy.14 = bf16[512,256]{1,0:T(8,128)(2,1)} copy(bf16[512,256]{1,0:T(8,128)(2,1)S(1)} %get-tuple-element.3) | data formatting | bytes 524288
  64.3 0.7 copy.15
  65.0 0.7 copy.16

commit v3 on v2

--- a/solution.py
+++ b/solution.py
@@ -16,7 +16,7 @@
 WIDE = 256
 Y_TYPE = BF16
 X_TYPE = BF16
-X_SUM = F32
+X_SUM = BF16
 HOPS = ((4, 3), (3, 4))
 
 
@@ -38,7 +38,6 @@
     grad_up_ref,
     a_ref,
     g_ref,
-    w_ref,
     down_ref,
     up_ref,
     masked,
@@ -122,7 +121,6 @@
                 (up_hbm, up_ref),
                 (a_hbm, a_ref),
                 (down_hbm, down_ref),
-                (w_hbm, w_ref),
             )
         )
     ]
@@ -135,6 +133,92 @@
     for device in greeted:
         pl.semaphore_signal(barrier, inc=1, device_id=device, device_id_type=MESH)
 
+    pl.semaphore_wait(barrier, len(greeted))
+
+    def flip_of(xx, cc):
+        low = lax.rem(xx, 2)
+        return jnp.where(lax.div(xx, 2) == cc, low, 1 - low)
+
+    flip = flip_of(x, c)
+
+    def shard_of(j):
+        return 2 * c + lax.rem(j + flip, 2)
+
+    to_core = lax.div(x, 2)
+    pre = []
+    for j in range(2):
+        to_x = 2 * c + j
+        is_self = jnp.logical_and(to_x == x, to_core == c)
+        piece = w_hbm.at[:, pl.ds(j * WIDE, WIDE)]
+        spot = w_all.at[y, x]
+        chunk = lax.rem(x + flip_of(to_x, to_core), 2)
+        keep = pltpu.make_async_copy(piece, spot, pre_r.at[chunk])
+        move = pltpu.make_async_remote_copy(
+            src_ref=piece,
+            dst_ref=spot,
+            send_sem=pre_s.at[j],
+            recv_sem=pre_r.at[chunk],
+            device_id=at(y, to_core, z, to_x),
+            device_id_type=MESH,
+        )
+        pre.append((is_self, move))
+
+        @pl.when(is_self)
+        def _(keep=keep):
+            keep.start()
+
+        @pl.when(jnp.logical_not(is_self))
+        def _(move=move):
+            move.start()
+
+    m_copy, w_copy, sib_copy = {}, {}, {}
+
+    def m_hop(direction, half, hop):
+        owner = wrap(z - hop if direction == 0 else z + hop, NZ)
+        src = g_hbm.at[pl.ds(half * WIDE, WIDE)] if hop == 0 else m_all.at[owner, half]
+        m_copy[direction, half, hop] = send(
+            src,
+            m_all.at[owner, half],
+            m_s.at[direction, half, hop],
+            m_r.at[direction, half, hop],
+            z_next[direction],
+        )
+
+    def w_hop(direction, j, hop):
+        owner = wrap(y - hop if direction == 0 else y + hop, NY)
+        spot = w_all.at[owner, shard_of(j)]
+        w_copy[direction, j, hop] = send(
+            spot, spot, w_s.at[direction, j, hop], w_r.at[direction, j, hop], y_next[direction]
+        )
+
+    def to_sibling(owner, slot, j):
+        spot = w_all.at[owner, shard_of(j)]
+        sib_copy[slot, j] = send(spot, spot, sib_s.at[slot, j], sib_r.at[slot, j], sibling)
+
+    def w_slot(direction, hop):
+        return 7 if hop == 3 else 1 + 2 * hop + direction
+
+    def step(hop, j):
+        for direction in range(2):
+            last = HOPS[j][direction]
+            if hop >= last:
+                continue
+            m_copy[direction, j, hop].wait_recv()
+            if hop + 1 < last:
+                m_hop(direction, j, hop + 1)
+        for direction in range(2):
+            last = HOPS[j][direction]
+            if hop >= last:
+                continue
+            w_copy[direction, j, hop].wait_recv()
+            if hop + 1 < last:
+                w_hop(direction, j, hop + 1)
+            owner = wrap(y - 1 - hop if direction == 0 else y + 1 + hop, NY)
+            to_sibling(owner, w_slot(direction, hop), j)
+
+    for half in range(2):
+        for direction in range(2):
+            m_hop(direction, half, 0)
     tenants = [tenant_ref[grp * NB + b] for b in range(NB)]
     zeros = jnp.zeros((RANK, WIDE), BF16)
     contract_last = (((1,), (1,)), ((), ()))
@@ -162,86 +246,6 @@
         rank_part[b] = lax.dot_general(
             kept, ups, contract_last, preferred_element_type=F32
         ) + lax.dot_general(a_ref[rows, :], downs, contract_last, preferred_element_type=F32)
-    pl.semaphore_wait(barrier, len(greeted))
-
-    def flip_of(xx, cc):
-        low = lax.rem(xx, 2)
-        return jnp.where(lax.div(xx, 2) == cc, low, 1 - low)
-
-    flip = flip_of(x, c)
-
-    def shard_of(j):
-        return 2 * c + lax.rem(j + flip, 2)
-
-    to_core = lax.div(x, 2)
-    pre = []
-    for j in range(2):
-        to_x = 2 * c + j
-        is_self = jnp.logical_and(to_x == x, to_core == c)
-        piece = w_ref.at[:, pl.ds(j * WIDE, WIDE)]
-        spot = w_all.at[y, x]
-        chunk = lax.rem(x + flip_of(to_x, to_core), 2)
-        keep = pltpu.make_async_copy(piece, spot, pre_r.at[chunk])
-        move = pltpu.make_async_remote_copy(
-            src_ref=piece,
-            dst_ref=spot,
-            send_sem=pre_s.at[j],
-            recv_sem=pre_r.at[chunk],
-            device_id=at(y, to_core, z, to_x),
-            device_id_type=MESH,
-        )
-        pre.append((is_self, move))
-
-        @pl.when(is_self)
-        def _(keep=keep):
-            keep.start()
-
-        @pl.when(jnp.logical_not(is_self))
-        def _(move=move):
-            move.start()
-
-    m_copy, w_copy, sib_copy = {}, {}, {}
-
-    def m_hop(direction, half, hop):
-        owner = wrap(z - hop if direction == 0 else z + hop, NZ)
-        src = g_ref.at[pl.ds(half * WIDE, WIDE)] if hop == 0 else m_all.at[owner, half]
-        m_copy[direction, half, hop] = send(
-            src,
-            m_all.at[owner, half],
-            m_s.at[direction, half, hop],
-            m_r.at[direction, half, hop],
-            z_next[direction],
-        )
-
-    def w_hop(direction, j, hop):
-        owner = wrap(y - hop if direction == 0 else y + hop, NY)
-        spot = w_all.at[owner, shard_of(j)]
-        w_copy[direction, j, hop] = send(
-            spot, spot, w_s.at[direction, j, hop], w_r.at[direction, j, hop], y_next[direction]
-        )
-
-    def to_sibling(owner, slot, j):
-        spot = w_all.at[owner, shard_of(j)]
-        sib_copy[slot, j] = send(spot, spot, sib_s.at[slot, j], sib_r.at[slot, j], sibling)
-
-    def w_slot(direction, hop):
-        return 7 if hop == 3 else 1 + 2 * hop + direction
-
-    def step(hop):
-        for j in range(2):
-            for direction in range(2):
-                last = HOPS[j][direction]
-                if hop >= last:
-                    continue
-                w_copy[direction, j, hop].wait_recv()
-                if hop + 1 < last:
-                    w_hop(direction, j, hop + 1)
-                owner = wrap(y - 1 - hop if direction == 0 else y + 1 + hop, NY)
-                to_sibling(owner, w_slot(direction, hop), j)
-                m_copy[direction, j, hop].wait_recv()
-                if hop + 1 < last:
-                    m_hop(direction, j, hop + 1)
-
     rx = []
     for k in range(1, NX):
         rx.append(
@@ -253,12 +257,9 @@
                 x_peer[k - 1],
             )
         )
-    for half in range(2):
-        for direction in range(2):
-            m_hop(direction, half, 0)
     for j in range(2):
         pltpu.make_async_copy(
-            w_ref.at[:, pl.ds(0, WIDE)], w_all.at[y, shard_of(j)], pre_r.at[j]
+            w_hbm.at[:, pl.ds(0, WIDE)], w_all.at[y, shard_of(j)], pre_r.at[j]
         ).wait()
         for direction in range(2):
             w_hop(direction, j, 0)
@@ -317,11 +318,8 @@
                 z_peer[k - 1],
             )
         )
-    step(0)
-    for copy in own:
-        copy.wait()
-    arrived(-1)
-    products(0)
+    step(0, 0)
+    step(0, 1)
     for copy in rz:
         copy.wait_recv()
     total = rank_mid[z]
@@ -339,9 +337,11 @@
                 z_peer[k - 1],
             )
         )
-    step(1)
-    arrived(0)
-    products(1)
+    for copy in own:
+        copy.wait()
+    arrived(-1)
+    products(0)
+    step(1, 0)
     for copy in gz:
         copy.wait_recv()
     gx = []
@@ -351,9 +351,9 @@
                 rank_all.at[x], rank_all.at[x], gx_s.at[k - 1], gx_r.at[k - 1], x_peer[k - 1]
             )
         )
-    step(2)
-    arrived(1)
-    products(2)
+    step(1, 1)
+    arrived(0)
+    products(1)
     for copy in gx:
         copy.wait_recv()
 
@@ -371,11 +371,7 @@
     swap = send(
         panels.at[pl.ds(0, NB)], panels.at[pl.ds(NB, NB)], pan_s, pan_r, sibling
     )
-    for b in range(NB):
-        rows = pl.ds(b * BLOCK, BLOCK)
-        ranks = rank_all[b].reshape(BLOCK, BLOCK)
-        downs = jnp.concatenate([down_ref[tenants[b]], zeros], axis=0)
-        adapter[rows, :] = SCALE * jnp.dot(ranks, downs, preferred_element_type=F32)
+    step(2, 0)
 
     my_places = [place_ref[tenants[b]] for b in range(NB)]
     sib_places = [place_ref[tenant_ref[sib_grp * NB + b]] for b in range(NB)]
@@ -416,22 +412,25 @@
     for slot in range(2):
         for direction in range(2):
             y_hop(direction, slot, 0)
-    step(3)
+    step(2, 1)
+    arrived(1)
+    products(2)
+    y_step(0)
+    step(3, 0)
+    step(3, 1)
     arrived(2)
     products(3)
+
+    @pl.when(y != z)
+    def _():
+        for shard in range(NX):
+            multiply(wrap(z + 4, NZ), shard)
+
     arrived(3)
     x_next = (x_peer[0], x_peer[2])
     x_at = (wrap(x + 1, NX), wrap(x - 1, NX))
     opposite = wrap(x + 2, NX)
     x_copy = {}
-
-    for shard in range(NX):
-        multiply(wrap(y + 4, NY), shard)
-
-    @pl.when(y != z)
-    def _():
-        for shard in range(NX):
-            multiply(wrap(z + 4, NZ), shard)
 
     def x_send(kind, direction, sub, src, dst):
         x_copy[kind, direction, sub] = send(
@@ -442,17 +441,26 @@
             x_next[direction],
         )
 
+    last_chip = wrap(y + 4, NY)
+    multiply(last_chip, opposite)
     for sub in range(2):
         for direction in range(2):
             rows = pl.ds(direction * WIDE + sub * BLOCK, BLOCK)
             x_out[0, direction, sub] = partial[opposite, rows, :].astype(X_TYPE)
             x_send(0, direction, sub, x_out.at[0, direction, sub], x_relay.at[direction, sub])
+    y_step(1)
+    for shard in (x_at[0], x_at[1], x):
+        multiply(last_chip, shard)
     for direction in range(2):
         for sub in range(2):
             rows = pl.ds((1 - direction) * WIDE + sub * BLOCK, BLOCK)
             x_out[1, direction, sub] = partial[x_at[direction], rows, :].astype(X_TYPE)
             x_send(1, direction, sub, x_out.at[1, direction, sub], x_direct.at[direction, sub])
-    y_step(0)
+    for b in range(NB):
+        rows = pl.ds(b * BLOCK, BLOCK)
+        ranks = rank_all[b].reshape(BLOCK, BLOCK)
+        downs = jnp.concatenate([down_ref[tenants[b]], zeros], axis=0)
+        adapter[rows, :] = SCALE * jnp.dot(ranks, downs, preferred_element_type=F32)
     for sub in range(2):
         for direction in range(2):
             x_copy[0, direction, sub].wait_recv()
@@ -460,8 +468,8 @@
             value = x_relay[direction, sub].astype(F32) + partial[x_at[direction], rows, :]
             x_sum[direction, sub] = value.astype(X_SUM)
             x_send(2, direction, sub, x_sum.at[direction, sub], x_far.at[direction, sub])
-    y_step(1)
-    y_step(2)
+        if sub == 0:
+            y_step(2)
     for direction in range(2):
         for sub in range(2):
             x_copy[1, direction, sub].wait_recv()
@@ -523,7 +531,6 @@
             scratch_shapes=[
                 pltpu.VMEM((NB * BLOCK, WIDE), BF16),
                 pltpu.VMEM((NB * BLOCK, WIDE), BF16),
-                pltpu.VMEM((WIDE, 2 * WIDE), BF16),
                 pltpu.VMEM(down.shape, BF16),
                 pltpu.VMEM(up.shape, BF16),
                 pltpu.VMEM((NB * BLOCK, WIDE), BF16),
@@ -567,7 +574,7 @@
                 dma((3, 2, 2)),
                 dma((3, 2, 2)),
                 dma((2,)),
-                dma((5,)),
+                dma((4,)),
             ],
             compiler_params=pltpu.CompilerParams(
                 collective_id=0, has_side_effects=True, vmem_limit_bytes=56 << 20

time: 65.8 us -> 64 us (0.973)
  the two profiles are of different devices: /device:TPU:16 before, /device:TPU:25 now
where the time goes in v3:
time: 64 us; the launch traced here: 63.8 us
  Pallas kernels  61.2 us (96%)
  local copies, waits for them, and re-layouts  2.01 us (3%)
  between operations  0.64 us (1%)
    pallas_call x1, Pallas kernels, whole(): pl.pallas_call(kernel, out_shape=(pltpu.VMEM((NB * BLOCK, WIDE), BF16), p...  61.2 us
    unnamed x3, local copies, waits for them, and re-layouts  2.01 us

profile of v3, /device:TPU:25, one launch (start us, length us, event | category | flops | bytes accessed | tf_op | source)
XLA Modules:
  0.0 63.8 jit_solution(2720184246100027749)
XLA Ops:
  0.6 61.2 %shard_map.103 = (bf16[512,256]{1,0:T(8,128)(2,1)S(1)}, f32[2,64,256]{2,1,0:T(8,128)S(1)}, f32[2,64,256]{2,1,0:T(8,128)S(1)}) custom-call(s32[64]{0:T(128)} %tenant_ref.1, s32[64]{0:T(128)} %valid_ref.1, s32[32]{0:T(128)} %place_ref.1, bf16[512,256]{1,0:T(8,128)(2,1)} %a_hbm.1, bf16[512,256]{1,0:T(8,128)(2,1)} %g_hbm.1, bf16[256,512]{1,0:T(8,128)(2,1)} %w_hbm.1, ...), custom_call_target="tpu_custom_call" | custom-call | tf_op jit(solution)/shard_map/pallas_call | solution.py:522
  61.8 0.7 %copy.14 = bf16[512,256]{1,0:T(8,128)(2,1)} copy(bf16[512,256]{1,0:T(8,128)(2,1)S(1)} %get-tuple-element.3) | data formatting | bytes 524288
  62.5 0.7 %copy.15 = f32[2,64,256]{2,1,0:T(8,128)} copy(f32[2,64,256]{2,1,0:T(8,128)S(1)} %get-tuple-element.4) | data formatting | bytes 262144
  63.2 0.7 %copy.16 = f32[2,64,256]{2,1,0:T(8,128)} copy(f32[2,64,256]{2,1,0:T(8,128)S(1)} %get-tuple-element.5) | data formatting | bytes 262144
